TPU v7x, 256 devices: a whole 4x4x8 slice. The times are simulated.
256 devices in a mesh: row: 16 (over x, z_lo), col: 16 (over z_hi, y, core).
Axes of the slice: x: 4, y: 4, z: 8 (z_hi: 2, z_lo: 4; z = z_hi * 4 + z_lo), core: 2. Of those that a mesh axis runs over, the one named last changes fastest.
Arguments:
- acts: bfloat16 [2048, 5120], P('col', 'row'), may hold values from -60 to 60
- out_grads: bfloat16 [2048, 13824], P('row', 'col'), may hold values from -0.06187184 to 0.06187184
- momentum: float32 [5120, 13824], P('row', 'col'), may hold values from -200 to 200
- weight: float32 [5120, 13824], P('row', 'col'), may hold values from -0.078125 to 0.078125
Outputs:
- momentum_new: float32 [5120, 13824], P('row', 'col')
- update: bfloat16 [5120, 13824], P('row', 'col')
- weight_new: float32 [5120, 13824], P('row', 'col')
All inputs are finite; a program needn't handle non-finite values.
Results may differ from a plain program's by a relative error of at most 0.014.
Values may be sent and summed in bfloat16 or wider, within the bound.
A program may use at most 64 MiB of HBM per device.

v0:
```python
import math
import jax
import jax.numpy as jnp
from jax import lax
from jax.sharding import PartitionSpec as P

D = 5120


def body(acts, out_grads, momentum, weight):
    token_acts = lax.all_gather(acts, "col", axis=0, tiled=True)
    slab_rows = token_acts
    gradient = lax.dot_general(
        slab_rows,
        lax.all_gather(out_grads, "row", axis=0, tiled=True),
        (((0,), (0,)), ((), ())),
        preferred_element_type=jnp.float32,
    )
    momentum_new = 0.95 * momentum + gradient
    blended = gradient + 0.95 * momentum_new
    rounded = blended.astype(jnp.bfloat16)
    col_panel = lax.all_gather(rounded, "row", axis=0, tiled=True)
    slab_rows = col_panel
    gram_tile = lax.psum_scatter(
        lax.dot_general(
            slab_rows, rounded, (((1,), (1,)), ((), ())), preferred_element_type=jnp.float32
        ).astype(jnp.bfloat16),
        "col",
        scatter_dimension=0,
        tiled=True,
    )
    gram_cols = lax.all_gather(gram_tile, "col", axis=0, tiled=True)
    gram_rows = lax.all_gather(gram_tile, "row", axis=1, tiled=True)
    gram_square = jnp.dot(gram_rows, gram_cols, preferred_element_type=jnp.float32)
    total_sum = lax.psum(jnp.sum(gram_square * gram_square), ("row", "col"))
    schatten = jnp.sqrt(total_sum + 1e-06)
    square_root = jnp.sqrt(schatten)
    fourth_root = jnp.sqrt(square_root)
    poly_tile = (
        -4.775 * gram_tile.astype(jnp.float32) / square_root + 2.0315 * gram_square / schatten
    ).astype(jnp.bfloat16)
    poly_cols = lax.all_gather(poly_tile, "col", axis=0, tiled=True)
    product = lax.dot_general(
        poly_cols, col_panel, (((0,), (0,)), ((), ())), preferred_element_type=jnp.float32
    )
    orthogonal = (3.4445 * rounded.astype(jnp.float32) + product) / fourth_root
    factor = math.sqrt(D)
    update = (factor * orthogonal).astype(jnp.bfloat16)
    weight_new = 0.998 * weight - 0.02 * factor * orthogonal
    return (momentum_new, update, weight_new)


def solution(mesh):
    in_specs = (P("col", "row"), P("row", "col"), P("row", "col"), P("row", "col"))
    out_specs = (P("row", "col"), P("row", "col"), P("row", "col"))
    return jax.shard_map(body, mesh=mesh, in_specs=in_specs, out_specs=out_specs, check_vma=False)
```

profile of v0, /device:TPU:1, one launch (start us, length us, event | category | flops | bytes accessed | tf_op | source)
XLA Modules:
  0.0 829.8 jit_solution(14348969872725976175)
XLA Ops:
  7.2 0.0 all-gather.7.cloned.1.call-start
  7.2 0.7 all-gather.7.cloned.1.call-update
  7.9 0.0 all-gather.9.cloned.1.call-start
  7.9 0.7 all-gather.9.cloned.1.call-update
  8.6 0.0 all-gather.11.cloned.1.call-start
  8.7 63.7 %all-gather.7.cloned.1.call-done = bf16[2048,320]{0,1:T(8,128)(2,1)} async-done(((bf16[128,320]{0,1:T(8,128)(2,1)}), bf16[2048,320]{0,1:T(8,128)(2,1)}) %all-gather.7.cloned.1.call-update) | async-done | bytes 1310736 | tf_op jit(solution)/shard_map/all_gather | solution.py:11
  72.4 90.5 %all-gather.9.cloned.1.call-done = bf16[2048,864]{0,1:T(8,128)(2,1)} async-done(((bf16[128,864]{0,1:T(8,128)(2,1)}), bf16[2048,864]{0,1:T(8,128)(2,1)}) %all-gather.9.cloned.1.call-update) | async-done | bytes 3538960 | tf_op jit(solution)/shard_map/all_gather | solution.py:15
  162.9 5.5 add_convert_fusion
  168.4 0.0 all-gather.11.cloned.1.call-update
  168.4 0.0 reduce-scatter.2.cloned.1.call-start
  168.4 210.8 %all-gather.11.cloned.1.call-done = bf16[5120,864]{1,0:T(8,128)(2,1)} async-done(((bf16[320,864]{1,0:T(8,128)(2,1)}), bf16[5120,864]{1,0:T(8,128)(2,1)}) %all-gather.11.cloned.1.call-update) | async-done | bytes 8847376 | tf_op jit(solution)/shard_map/all_gather | solution.py:22
  379.3 9.3 %convolution_convert_fusion = bf16[5120,320]{1,0:T(8,128)(2,1)} fusion(bf16[5120,864]{1,0:T(8,128)(2,1)} %all-gather.11.cloned.1.call-done, bf16[320,864]{1,0:T(8,128)(2,1)} %get-tuple-element.3), kind=kOutput, calls=%fused_computation | convolution fusion | flops 2832793600 | bytes 12677120 | tf_op jit(solution)/shard_map/dot_general | solution.py:25
  388.5 0.0 reduce-scatter.2.cloned.1.call-update
  388.6 0.0 all-gather.15.cloned.1.call-start
  388.6 98.2 %reduce-scatter.2.cloned.1.call-done = bf16[320,320]{1,0:T(8,128)(2,1)} async-done(((bf16[5120,320]{1,0:T(8,128)(2,1)}), bf16[320,320]{1,0:T(8,128)(2,1)}) %reduce-scatter.2.cloned.1.call-update) | async-done | bytes 204816 | tf_op jit(solution)/shard_map/reduce_scatter | solution.py:24
  486.8 0.0 all-gather.15.cloned.1.call-update
  486.8 0.0 all-gather.13.cloned.1.call-start
  486.9 1.8 copy.7
  488.7 0.0 all-gather.13.cloned.1.call-update
  488.7 0.0 copy-start
  488.7 0.0 copy-start.1
  488.7 0.0 copy-start.2
  488.7 0.0 all-gather.17.cloned.1.call-start
  488.8 74.5 %all-gather.15.cloned.1.call-done = bf16[5120,320]{1,0:T(8,128)(2,1)} async-done(((bf16[320,320]{1,0:T(8,128)(2,1)}), bf16[5120,320]{1,0:T(8,128)(2,1)}) %all-gather.15.cloned.1.call-update) | async-done | bytes 3276816 | tf_op jit(solution)/shard_map/all_gather | solution.py:32
  563.2 93.3 %all-gather.13.cloned.1.call-done = bf16[320,5120]{0,1:T(8,128)(2,1)} async-done(((bf16[320,320]{0,1:T(8,128)(2,1)}), bf16[320,5120]{0,1:T(8,128)(2,1)}) %all-gather.13.cloned.1.call-update) | async-done | bytes 3276816 | tf_op jit(solution)/shard_map/all_gather | solution.py:33
  656.5 5.8 multiply_reduce_fusion
  662.3 77.1 %psum.7 = f32[]{:T(128)} all-reduce(f32[]{:T(128)} %get-tuple-element.7), channel_id=1, replica_groups=mesh['row'=16,'col'=16] {'row','col'}, use_global_device_ids=true, to_apply=%region_2.0 | all-reduce | flops 1 | bytes 8 | tf_op jit(solution)/shard_map/psum | solution.py:35
  740.2 0.0 copy-done
  740.2 0.8 add_convert_fusion.1
  741.0 0.0 all-gather.17.cloned.1.call-update
  741.1 72.2 %all-gather.17.cloned.1.call-done = bf16[5120,320]{1,0:T(8,128)(2,1)} async-done(((bf16[320,320]{1,0:T(8,128)(2,1)}), bf16[5120,320]{1,0:T(8,128)(2,1)}) %all-gather.17.cloned.1.call-update) | async-done | bytes 3276816 | tf_op jit(solution)/shard_map/all_gather | solution.py:42
  813.3 0.0 copy-done.1
  813.3 0.0 copy-done.2
  813.3 9.7 %multiply_subtract_fusion = (f32[320,864]{1,0:T(8,128)}, bf16[320,864]{1,0:T(8,128)(2,1)}) fusion(f32[320,864]{1,0:T(8,128)S(1)} %copy-done.2, f32[]{:T(128)S(6)} %sqrt.11, bf16[5120,320]{1,0:T(8,128)(2,1)} %all-gather.17.cloned.1.call-done, bf16[5120,864]{1,0:T(8,128)(2,1)} %all-gather.11.cloned.1.call-done, bf16[320,864]{1,0:T(8,128)(2,1)S(1)} %copy-done.1), kind=kOutput, calls=%fused_computation.3 | convolution fusion | flops 2833643520 | bytes 15441924 | tf_op jit(solution)/shard_map/dot_general | solution.py:43
Async XLA Ops:
  7.2 65.2 %all-gather.7.cloned.1.call-start = ((), (), s32[]{:S(2)}) async-start(), calls=%async_computation.1 | async-start | bytes 1392640 | tf_op jit(solution)/shard_map/all_gather | solution.py:11
  7.9 155.0 %all-gather.9.cloned.1.call-start = ((), (), s32[]{:S(2)}) async-start(), calls=%async_computation.2 | async-start | bytes 3760128 | tf_op jit(solution)/shard_map/all_gather | solution.py:15
  8.6 370.6 %all-gather.11.cloned.1.call-start = ((), (), s32[]{:S(2)}) async-start(), calls=%async_computation.3 | async-start | bytes 9748480 | tf_op jit(solution)/shard_map/all_gather | solution.py:22
  168.4 318.4 %reduce-scatter.2.cloned.1.call-start = ((), (), s32[]{:S(2)}) async-start(), calls=%async_computation.4 | async-start | bytes 4177920 | tf_op jit(solution)/shard_map/reduce_scatter | solution.py:24
  388.6 174.7 %all-gather.15.cloned.1.call-start = ((), (), s32[]{:S(2)}) async-start(), calls=%async_computation.6 | async-start | bytes 4177920 | tf_op jit(solution)/shard_map/all_gather | solution.py:32
  486.8 169.7 %all-gather.13.cloned.1.call-start = ((), (), s32[]{:S(2)}) async-start(), calls=%async_computation.5 | async-start | bytes 4177920 | tf_op jit(solution)/shard_map/all_gather | solution.py:33
  488.7 251.5 %copy-start = (bf16[320,320]{1,0:T(8,128)(2,1)S(1)}, bf16[320,320]{1,0:T(8,128)(2,1)}, u32[]{:S(2)}) copy-start(bf16[320,320]{1,0:T(8,128)(2,1)} %reduce-scatter.2.cloned.1.call-done) | copy-start | bytes 614404
  488.7 324.6 %copy-start.1 = (bf16[320,864]{1,0:T(8,128)(2,1)S(1)}, bf16[320,864]{1,0:T(8,128)(2,1)}, u32[]{:S(2)}) copy-start(bf16[320,864]{1,0:T(8,128)(2,1)} %get-tuple-element.3) | copy-start | bytes 1658884
  488.7 324.6 %copy-start.2 = (f32[320,864]{1,0:T(8,128)S(1)}, f32[320,864]{1,0:T(8,128)}, u32[]{:S(2)}) copy-start(f32[320,864]{1,0:T(8,128)} %param.7) | copy-start | bytes 3317764
  488.7 324.5 %all-gather.17.cloned.1.call-start = ((), (), s32[]{:S(2)}) async-start(), calls=%async_computation.7 | async-start | bytes 4177920 | tf_op jit(solution)/shard_map/all_gather | solution.py:42
Sparse Core Ops, SparseCore 0:
  10.5 61.8 all-gather.6
  74.1 88.7 all-gather.8
  168.5 210.7 all-gather.10
  388.7 98.0 reduce-scatter.1
  489.4 73.8 all-gather.14
  565.5 91.0 all-gather.12
  741.1 72.0 all-gather.16
where the time goes:
time: 830 us
  waiting for transfers between devices  705 us (85%)
  blocking collectives  77.1 us (9%)
  matrix products  30.3 us (4%)
  between operations  14.9 us (2%)
    all_gather x1, waiting for transfers between devices, body(): col_panel = lax.all_gather(rounded, 'row', axis=0, tiled=True)  211 us
    reduce_scatter x1, waiting for transfers between devices, body(): lax.psum_scatter(lax.dot_general(slab_rows, rounded, (((1,), (1,)), ((),...  98.2 us
    all_gather x1, waiting for transfers between devices, body(): gram_rows = lax.all_gather(gram_tile, 'row', axis=1, tiled=True)  93.3 us
    all_gather x1, waiting for transfers between devices, body(): lax.all_gather(out_grads, 'row', axis=0, tiled=True)  90.5 us
    psum x1, blocking collectives, body(): total_sum = lax.psum(jnp.sum(gram_square * gram_square), ('row', 'col'))  77.1 us
    all_gather x1, waiting for transfers between devices, body(): gram_cols = lax.all_gather(gram_tile, 'col', axis=0, tiled=True)  74.5 us
    all_gather x1, waiting for transfers between devices, body(): poly_cols = lax.all_gather(poly_tile, 'col', axis=0, tiled=True)  72.2 us
    all_gather x1, waiting for transfers between devices, body(): token_acts = lax.all_gather(acts, 'col', axis=0, tiled=True)  63.7 us
  transfers between devices with their start and end apart: 7, of which 7 were waited for; matrix products, arithmetic and copies ran while one was open for 0% of the time, Pallas kernels for 0%

commit v1 on v0

--- a/solution.py
+++ b/solution.py
@@ -29,7 +29,9 @@
         scatter_dimension=0,
         tiled=True,
     )
-    gram_cols = lax.all_gather(gram_tile, "col", axis=0, tiled=True)
+    gram_cols = jnp.concatenate(
+        lax.all_to_all(jnp.stack([gram_tile] * lax.axis_size("col")), "col", 0, 0), axis=0
+    )
     gram_rows = lax.all_gather(gram_tile, "row", axis=1, tiled=True)
     gram_square = jnp.dot(gram_rows, gram_cols, preferred_element_type=jnp.float32)
     total_sum = lax.psum(jnp.sum(gram_square * gram_square), ("row", "col"))

time: 830 us -> 840 us (1.012)
    all_to_all x0 -> x1, waiting for transfers between devices: none -> 96.6 us  [body(): lax.all_to_all(jnp.stack([gram_tile] * lax.axis_size('col')), 'col', 0, 0)]
    all_gather x1 -> x0, waiting for transfers between devices: 74.5 us -> none  [body(): gram_cols = lax.all_gather(gram_tile, 'col', axis=0, tiled=True)]
    all_gather x1, waiting for transfers between devices: 93.3 us -> 67.6 us  [body(): gram_rows = lax.all_gather(gram_tile, 'row', axis=1, tiled=True)]
where the time goes in v1:
time: 840 us; the launch traced here: 839 us
  waiting for transfers between devices  700 us (83%)
  blocking collectives  82.2 us (10%)
  matrix products  30.4 us (4%)
  between operations  14.9 us (2%)
    all_gather x1, waiting for transfers between devices, body(): col_panel = lax.all_gather(rounded, 'row', axis=0, tiled=True)  211 us
    reduce_scatter x1, waiting for transfers between devices, body(): lax.psum_scatter(lax.dot_general(slab_rows, rounded, (((1,), (1,)), ((),...  98.2 us
    all_to_all x1, waiting for transfers between devices, body(): lax.all_to_all(jnp.stack([gram_tile] * lax.axis_size('col')), 'col', 0, 0)  96.6 us
    all_gather x1, waiting for transfers between devices, body(): lax.all_gather(out_grads, 'row', axis=0, tiled=True)  90.5 us
    psum x1, blocking collectives, body(): total_sum = lax.psum(jnp.sum(gram_square * gram_square), ('row', 'col'))  82.2 us
    all_gather x1, waiting for transfers between devices, body(): poly_cols = lax.all_gather(poly_tile, 'col', axis=0, tiled=True)  70.7 us
    all_gather x1, waiting for transfers between devices, body(): gram_rows = lax.all_gather(gram_tile, 'row', axis=1, tiled=True)  67.6 us
    all_gather x1, waiting for transfers between devices, body(): token_acts = lax.all_gather(acts, 'col', axis=0, tiled=True)  63.7 us
  transfers between devices with their start and end apart: 7, of which 7 were waited for; matrix products, arithmetic and copies ran while one was open for 0% of the time, Pallas kernels for 0%

profile of v1, /device:TPU:1, one launch (start us, length us, event | category | flops | bytes accessed | tf_op | source)
XLA Modules:
  0.0 839.5 jit_solution(12469018511275036384)
XLA Ops:
  7.2 0.0 all-gather.6.cloned.1.call-start
  7.2 0.7 all-gather.6.cloned.1.call-update
  7.9 0.0 all-gather.8.cloned.1.call-start
  7.9 0.7 all-gather.8.cloned.1.call-update
  8.6 0.0 all-gather.10.cloned.1.call-start
  8.7 63.7 %all-gather.6.cloned.1.call-done = bf16[2048,320]{0,1:T(8,128)(2,1)} async-done(((bf16[128,320]{0,1:T(8,128)(2,1)}), bf16[2048,320]{0,1:T(8,128)(2,1)}) %all-gather.6.cloned.1.call-update) | async-done | bytes 1310736 | tf_op jit(solution)/shard_map/all_gather | solution.py:11
  72.4 90.5 %all-gather.8.cloned.1.call-done = bf16[2048,864]{0,1:T(8,128)(2,1)} async-done(((bf16[128,864]{0,1:T(8,128)(2,1)}), bf16[2048,864]{0,1:T(8,128)(2,1)}) %all-gather.8.cloned.1.call-update) | async-done | bytes 3538960 | tf_op jit(solution)/shard_map/all_gather | solution.py:15
  162.9 5.5 add_convert_fusion
  168.4 0.0 all-gather.10.cloned.1.call-update
  168.4 0.0 reduce-scatter.2.cloned.1.call-start
  168.4 210.8 %all-gather.10.cloned.1.call-done = bf16[5120,864]{1,0:T(8,128)(2,1)} async-done(((bf16[320,864]{1,0:T(8,128)(2,1)}), bf16[5120,864]{1,0:T(8,128)(2,1)}) %all-gather.10.cloned.1.call-update) | async-done | bytes 8847376 | tf_op jit(solution)/shard_map/all_gather | solution.py:22
  379.3 9.2 %convolution_convert_fusion = bf16[5120,320]{1,0:T(8,128)(2,1)} fusion(bf16[5120,864]{1,0:T(8,128)(2,1)} %all-gather.10.cloned.1.call-done, bf16[320,864]{1,0:T(8,128)(2,1)} %get-tuple-element.3), kind=kOutput, calls=%fused_computation | convolution fusion | flops 2832793600 | bytes 12677120 | tf_op jit(solution)/shard_map/dot_general | solution.py:25
  388.5 0.0 reduce-scatter.2.cloned.1.call-update
  388.5 98.2 %reduce-scatter.2.cloned.1.call-done = bf16[320,320]{1,0:T(8,128)(2,1)} async-done(((bf16[5120,320]{1,0:T(8,128)(2,1)}), bf16[320,320]{1,0:T(8,128)(2,1)}) %reduce-scatter.2.cloned.1.call-update) | async-done | bytes 204816 | tf_op jit(solution)/shard_map/reduce_scatter | solution.py:24
  486.8 3.3 stack.2
  490.1 0.0 copy-start
  490.1 7.1 all-to-all-start
  497.2 0.0 all-gather.12.cloned.1.call-start
  497.3 0.0 copy-done
  497.3 0.9 copy.7
  498.2 0.0 all-gather.12.cloned.1.call-update
  498.2 0.0 all-gather.14.cloned.1.call-start
  498.2 96.6 %all-to-all-done = bf16[16,320,320]{2,1,0:T(8,128)(2,1)} async-done(((bf16[16,320,320]{2,1,0:T(8,128)(2,1)}), bf16[16,320,320]{2,1,0:T(8,128)(2,1)}, u32[]{:S(2)}, u32[]{:S(2)}) %all-to-all-start) | async-done | bytes 3276832 | tf_op jit(solution)/shard_map/all_to_all | solution.py:33
  594.9 67.6 %all-gather.12.cloned.1.call-done = bf16[320,5120]{0,1:T(8,128)(2,1)} async-done(((bf16[320,320]{0,1:T(8,128)(2,1)}), bf16[320,5120]{0,1:T(8,128)(2,1)}) %all-gather.12.cloned.1.call-update) | async-done | bytes 3276816 | tf_op jit(solution)/shard_map/all_gather | solution.py:35
  662.4 0.0 copy-start.1
  662.4 0.0 copy-start.2
  662.5 6.0 multiply_reduce_fusion
  668.4 82.2 %psum.7 = f32[]{:T(128)} all-reduce(f32[]{:T(128)} %get-tuple-element.7), channel_id=1, replica_groups=mesh['row'=16,'col'=16] {'row','col'}, use_global_device_ids=true, to_apply=%region_2.0 | all-reduce | flops 1 | bytes 8 | tf_op jit(solution)/shard_map/psum | solution.py:37
  751.3 0.8 add_convert_fusion.1
  752.1 0.0 all-gather.14.cloned.1.call-update
  752.2 70.7 %all-gather.14.cloned.1.call-done = bf16[5120,320]{1,0:T(8,128)(2,1)} async-done(((bf16[320,320]{1,0:T(8,128)(2,1)}), bf16[5120,320]{1,0:T(8,128)(2,1)}) %all-gather.14.cloned.1.call-update) | async-done | bytes 3276816 | tf_op jit(solution)/shard_map/all_gather | solution.py:44
  822.9 0.0 copy-done.1
  822.9 0.0 copy-done.2
  822.9 9.7 %multiply_subtract_fusion = (f32[320,864]{1,0:T(8,128)}, bf16[320,864]{1,0:T(8,128)(2,1)}) fusion(f32[320,864]{1,0:T(8,128)S(1)} %copy-done.2, f32[]{:T(128)S(6)} %sqrt.11, bf16[5120,320]{1,0:T(8,128)(2,1)} %all-gather.14.cloned.1.call-done, bf16[5120,864]{1,0:T(8,128)(2,1)} %all-gather.10.cloned.1.call-done, bf16[320,864]{1,0:T(8,128)(2,1)S(1)} %copy-done.1), kind=kOutput, calls=%fused_computation.3 | convolution fusion | flops 2833643520 | bytes 15441924 | tf_op jit(solution)/shard_map/dot_general | solution.py:45
Async XLA Ops:
  7.2 65.2 %all-gather.6.cloned.1.call-start = ((), (), s32[]{:S(2)}) async-start(), calls=%async_computation.2 | async-start | bytes 1392640 | tf_op jit(solution)/shard_map/all_gather | solution.py:11
  7.9 155.0 %all-gather.8.cloned.1.call-start = ((), (), s32[]{:S(2)}) async-start(), calls=%async_computation.3 | async-start | bytes 3760128 | tf_op jit(solution)/shard_map/all_gather | solution.py:15
  8.6 370.6 %all-gather.10.cloned.1.call-start = ((), (), s32[]{:S(2)}) async-start(), calls=%async_computation.4 | async-start | bytes 9748480 | tf_op jit(solution)/shard_map/all_gather | solution.py:22
  168.4 318.4 %reduce-scatter.2.cloned.1.call-start = ((), (), s32[]{:S(2)}) async-start(), calls=%async_computation.5 | async-start | bytes 4177920 | tf_op jit(solution)/shard_map/reduce_scatter | solution.py:24
  490.1 7.2 copy-start
  490.1 104.8 %all-to-all-start = ((bf16[16,320,320]{2,1,0:T(8,128)(2,1)}), bf16[16,320,320]{2,1,0:T(8,128)(2,1)}, u32[]{:S(2)}, u32[]{:S(2)}) async-start(bf16[16,320,320]{2,1,0:T(8,128)(2,1)} %stack.2), calls=%async_computation.1 | async-start | bytes 7864320 | tf_op jit(solution)/shard_map/all_to_all | solution.py:33
  497.2 165.2 %all-gather.12.cloned.1.call-start = ((), (), s32[]{:S(2)}) async-start(), calls=%async_computation.6 | async-start | bytes 4177920 | tf_op jit(solution)/shard_map/all_gather | solution.py:35
  498.2 324.7 %all-gather.14.cloned.1.call-start = ((), (), s32[]{:S(2)}) async-start(), calls=%async_computation.7 | async-start | bytes 4177920 | tf_op jit(solution)/shard_map/all_gather | solution.py:44
  662.4 160.5 %copy-start.1 = (bf16[320,864]{1,0:T(8,128)(2,1)S(1)}, bf16[320,864]{1,0:T(8,128)(2,1)}, u32[]{:S(2)}) copy-start(bf16[320,864]{1,0:T(8,128)(2,1)} %get-tuple-element.3) | copy-start | bytes 1658884
  662.4 160.5 %copy-start.2 = (f32[320,864]{1,0:T(8,128)S(1)}, f32[320,864]{1,0:T(8,128)}, u32[]{:S(2)}) copy-start(f32[320,864]{1,0:T(8,128)} %param.7) | copy-start | bytes 3317764
Sparse Core Ops, SparseCore 0:
  10.5 61.8 all-gather.5
  74.1 88.7 all-gather.7
  168.5 210.7 all-gather.9
  388.7 98.0 reduce-scatter.1
  500.1 162.2 all-gather.11
  752.3 70.5 all-gather.13
